TPU v7x, 32 devices: a whole 2x2x4 slice. The times are simulated.
32 devices in a mesh: lat: 4 (over y, core), lon: 8 (over z, x).
Axes of the slice: x: 2, y: 2, z: 4, core: 2. Of those that a mesh axis runs over, the one named last changes fastest.
Arguments:
- queries: bfloat16 [64, 128, 512], P('lat', 'lon'), may hold values from -6 to 6
- keys: bfloat16 [64, 128, 512], P('lat', 'lon'), may hold values from -6 to 6
- values: bfloat16 [64, 128, 512], P('lat', 'lon'), may hold values from -16 to 16
- rel_bias: float32 [8, 13, 13], replicated, may hold values from -4 to 4
- out_weight: bfloat16 [512, 1024], replicated, may hold values from -0.25 to 0.25
- cotangent: bfloat16 [64, 128, 1024], P('lat', 'lon'), may hold values from -16 to 16
Outputs:
- block_out: bfloat16 [64, 128, 1024], P('lat', 'lon')
- query_grad: bfloat16 [64, 128, 512], P('lat', 'lon')
- key_grad: bfloat16 [64, 128, 512], P('lat', 'lon')
- value_grad: bfloat16 [64, 128, 512], P('lat', 'lon')
- weight_grad: bfloat16 [512, 1024], replicated
- bias_grad: float32 [8, 13, 13], replicated
All inputs are finite; a program needn't handle non-finite values.
Results may differ from a plain program's by a relative error of at most 0.007.
Values may be sent and summed in bfloat16 or wider, within the bound.
No kernel may reach another device: no remote copies, remote signals or barrier semaphores. Data moves between devices by JAX's collectives and lax.ppermute only.
A program may use at most 128 MiB of HBM per device.

v0:
```python
import jax
import jax.numpy as jnp
from jax import lax
from jax.sharding import PartitionSpec as P

RAD = 6


def with_halo(block, sides, width, periodic):
    for axis, dim in sides:
        count = lax.axis_size(axis)
        forward = [(i, i + 1) for i in range(count - 1)]
        if periodic:
            forward.append((count - 1, 0))
        backward = [(target, source) for source, target in forward]
        low = lax.ppermute(
            lax.slice_in_dim(block, block.shape[dim] - width, None, axis=dim), axis, forward
        )
        high = lax.ppermute(lax.slice_in_dim(block, 0, width, axis=dim), axis, backward)
        block = jnp.concatenate([low, block, high], axis=dim)
    return block


def from_behind(block, axis, distance):
    devices = range(lax.axis_size(axis))
    route = [(i - distance, i) for i in devices if i - distance in devices]
    return lax.ppermute(block, axis, route)


def from_behind_2(value, axis, steps):
    count = lax.axis_size(axis)
    pairs = [(source, (source + steps) % count) for source in range(count)]
    return lax.ppermute(value, axis, pairs)


def relative_table(count_query, count_key):
    query_pos = jnp.arange(count_query, dtype=jnp.int32)
    key_pos = jnp.arange(count_key, dtype=jnp.int32)
    offset_pos = jnp.arange(2 * RAD + 1, dtype=jnp.int32)
    relative = key_pos[None, :] - query_pos[:, None]
    return (relative[:, :, None] == offset_pos[None, None, :]).astype(jnp.float32)


def shards(queries, keys, values, rel_bias, out_weight, cotangent):
    lat_dev, lon_dev, width = queries.shape
    heads = rel_bias.shape[0]
    head_size = width // heads
    outer_lat = lat_dev + 2 * RAD
    outer_lon = lon_dev + 2 * RAD
    count_query = lat_dev * lon_dev
    count_key = outer_lat * outer_lon
    tokens_all = count_query * lax.axis_size("lat") * lax.axis_size("lon")
    scale = head_size ** (-0.5)
    norm_factor = tokens_all ** (-0.5)
    paired = jnp.concatenate((keys, values), 2)
    widened = with_halo(paired, (("lon", 1),), RAD, True)
    outer = with_halo(widened, (("lat", 0),), RAD, False)
    outer_rows = outer.reshape(count_key, 2 * width)
    row_hot = relative_table(lat_dev, outer_lat)
    col_hot = relative_table(lon_dev, outer_lon)
    global_row = lax.axis_index("lat") * lat_dev + jnp.arange(outer_lat, dtype=jnp.int32) - RAD
    row_inside = ((global_row >= 0) & (global_row < lat_dev * lax.axis_size("lat"))).astype(
        jnp.float32
    )
    row_keep = row_hot * row_inside[None, :, None]
    bias_table = jnp.einsum(
        "hab,ika,jlb->hijkl", rel_bias, row_keep, col_hot, precision=lax.Precision.HIGHEST
    )
    keep_table = jnp.einsum("ika,jlb->ijkl", row_keep, col_hot, precision=lax.Precision.HIGHEST)
    keep_flat = keep_table.reshape(1, count_query, count_key) > 0.5
    masked_bias = jnp.where(keep_flat, bias_table.reshape(heads, count_query, count_key), -jnp.inf)
    query_heads = queries.reshape(count_query, heads, head_size).transpose(1, 0, 2)
    key_heads = outer_rows[:, :width].reshape(count_key, heads, head_size).transpose(1, 0, 2)
    value_heads = outer_rows[:, width:].reshape(count_key, heads, head_size).transpose(1, 0, 2)

    def weights_of(query_one, key_one, bias_one):
        scores = (
            lax.dot_general(
                query_one, key_one, (((1,), (1,)), ((), ())), preferred_element_type=jnp.float32
            )
            * scale
        )
        scores = scores + bias_one
        lifted = jnp.exp(scores - jnp.max(scores, -1, keepdims=True))
        return lifted / jnp.sum(lifted, -1, keepdims=True)

    def forward_head(items):
        query_one, key_one, value_one, bias_one = items
        probs = weights_of(query_one, key_one, bias_one)
        return jnp.dot(probs.astype(jnp.bfloat16), value_one, preferred_element_type=jnp.float32)

    mixed = lax.map(forward_head, (query_heads, key_heads, value_heads, masked_bias))
    attended = mixed.transpose(1, 0, 2).reshape(count_query, width).astype(jnp.bfloat16)
    block_out = jnp.dot(attended, out_weight, preferred_element_type=jnp.float32).astype(
        jnp.bfloat16
    )
    block_out = block_out.reshape(lat_dev, lon_dev, out_weight.shape[1])
    grad_rows = cotangent.reshape(count_query, cotangent.shape[2])
    attended_grad = lax.dot_general(
        grad_rows, out_weight, (((1,), (1,)), ((), ())), preferred_element_type=jnp.float32
    ).astype(jnp.bfloat16)
    weight_local = lax.dot_general(
        attended, grad_rows, (((0,), (0,)), ((), ())), preferred_element_type=jnp.float32
    )
    grad_heads = attended_grad.reshape(count_query, heads, head_size).transpose(1, 0, 2)

    def backward_head(items):
        query_one, key_one, value_one, grad_one, bias_one = items
        probs = weights_of(query_one, key_one, bias_one)
        rounded = probs.astype(jnp.bfloat16)
        slopes = lax.dot_general(
            grad_one, value_one, (((1,), (1,)), ((), ())), preferred_element_type=jnp.float32
        )
        inner_sum = jnp.sum(probs * slopes, -1, keepdims=True)
        score_grad = probs * (slopes - inner_sum)
        bias_part = jnp.einsum(
            "ijkl,ika,jlb->ab",
            score_grad.reshape(lat_dev, lon_dev, outer_lat, outer_lon),
            row_hot,
            col_hot,
            precision=lax.Precision.HIGHEST,
        )
        score_round = score_grad.astype(jnp.bfloat16)
        query_part = jnp.dot(score_round, key_one, preferred_element_type=jnp.float32) * scale
        key_part = (
            lax.dot_general(
                score_round, query_one, (((0,), (0,)), ((), ())), preferred_element_type=jnp.float32
            )
            * scale
        )
        value_part = lax.dot_general(
            rounded, grad_one, (((0,), (0,)), ((), ())), preferred_element_type=jnp.float32
        )
        return (query_part, key_part, value_part, bias_part)

    query_part, key_part, value_part, bias_local = lax.map(
        backward_head, (query_heads, key_heads, value_heads, grad_heads, masked_bias)
    )
    query_grad = query_part.transpose(1, 0, 2).reshape(lat_dev, lon_dev, width).astype(jnp.bfloat16)
    key_flat = key_part.transpose(1, 0, 2).reshape(count_key, width)
    value_flat = value_part.transpose(1, 0, 2).reshape(count_key, width)
    terms = jnp.concatenate((key_flat, value_flat), 1).reshape(outer_lat, outer_lon, 2 * width)
    top_rows = terms[:RAD]
    bottom_rows = terms[outer_lat - RAD :]
    middle = terms[RAD : RAD + lat_dev]
    from_below = from_behind(top_rows.astype(jnp.bfloat16), "lat", -1).astype(top_rows.dtype)
    from_above = from_behind(bottom_rows, "lat", 1)
    middle = middle.at[lat_dev - RAD :].add(from_below)
    middle = middle.at[:RAD].add(from_above)
    west_cols = middle[:, :RAD]
    east_cols = middle[:, outer_lon - RAD :]
    center = middle[:, RAD : RAD + lon_dev]
    from_east = from_behind_2(west_cols, "lon", -1)
    from_west = from_behind_2(east_cols, "lon", 1)
    center = center.at[:, lon_dev - RAD :].add(from_east)
    center = center.at[:, :RAD].add(from_west)
    key_grad = center[:, :, :width].astype(jnp.bfloat16)
    value_grad = center[:, :, width:].astype(jnp.bfloat16)
    weight_total, bias_total = lax.psum((weight_local, bias_local), ("lat", "lon"))
    weight_grad = (weight_total * norm_factor).astype(jnp.bfloat16)
    bias_grad = bias_total * norm_factor
    return (block_out, query_grad, key_grad, value_grad, weight_grad, bias_grad)


def solution(mesh):
    in_specs = (
        P("lat", "lon", None),
        P("lat", "lon", None),
        P("lat", "lon", None),
        P(),
        P(),
        P("lat", "lon", None),
    )
    out_specs = (
        P("lat", "lon", None),
        P("lat", "lon", None),
        P("lat", "lon", None),
        P("lat", "lon", None),
        P(),
        P(),
    )
    return jax.shard_map(shards, mesh=mesh, in_specs=in_specs, out_specs=out_specs, check_vma=False)
```

profile of v0, /device:TPU:0, one launch (start us, length us, event | category | flops | bytes accessed | tf_op | source)
XLA Modules:
  0.0 482.4 jit_solution(6144126483298326666)
XLA Ops:
  10.2 6.0 %collective-permute-start.1 = (bf16[16,6,1024]{2,1,0:T(8,128)(2,1)}, bf16[16,6,1024]{2,1,0:T(8,128)(2,1)S(1)}, u32[]{:S(2)}, u32[]{:S(2)}) collective-permute-start(bf16[16,6,1024]{2,1,0:T(8,128)(2,1)} %get-tuple-element.320), channel_id=1, source_target_pairs={{1,0},{2,1},{3,2},{4,3},{5,4},{6,5},{7,6},{0,7},{9,8},{10,9},{11,1... | collective-permute-start | bytes 589832 | tf_op jit(solution)/shard_map/ppermute | solution.py:19
  17.3 14.0 %convolution_bitcast_fusion.4 = f32[8,16,16,28,28]{4,3,2,0,1:T(8,128)S(1)} fusion(f32[16,28,8,13,1]{1,3,4,2,0:T(8,128)S(1)} %convolution_bitcast_fusion.5, s32[16,28]{1,0:T(8,128)S(1)} %iota_subtract_fusion), kind=kOutput, calls=%fused_computation.61 | convolution fusion | flops 250484416 | bytes 6610688 | tf_op jit(solution)/shard_map/hab,ika,jlb->hijkl/dot_general | solution.py:66
  31.3 13.2 %copy.37 = f32[8,16,16,28,28]{4,3,2,1,0:T(8,128)} copy(f32[8,16,16,28,28]{4,3,2,0,1:T(8,128)S(1)} %convolution_bitcast_fusion.4) | data formatting | bytes 12845056 | tf_op jit(solution)/shard_map/hab,ika,jlb->hijkl/transpose | solution.py:66
  44.6 28.1 %reshape.215 = f32[8,256,784]{2,1,0:T(8,128)} reshape(f32[8,16,16,28,28]{4,3,2,1,0:T(8,128)} %copy.37) | data formatting | bytes 12845056 | tf_op jit(solution)/shard_map/reshape | solution.py:71
  73.4 3.4 gt.20
  79.4 3.9 collective-permute-start.2
  83.3 6.6 %broadcast_select_fusion = f32[8,256,784]{2,1,0:T(8,128)} fusion(f32[8,256,784]{2,1,0:T(8,128)} %reshape.215, pred[256,784]{1,0:T(8,128)(4,1)S(1)} %gt.20), kind=kLoop, calls=%fused_computation.70 | loop fusion | flops 1605632 | bytes 13045760 | tf_op jit(solution)/shard_map/jit(_where)/select_n | solution.py:71
  91.1 8.2 %copy.41 = f32[8,256,784]{1,2,0:T(8,128)} copy(f32[8,256,784]{2,1,0:T(8,128)} %broadcast_select_fusion) | data formatting | bytes 12845056 | tf_op jit(solution)/shard_map/while | solution.py:92
  111.5 151.7 %while.34 = (s32[]{:T(128)}, bf16[8,256,64]{1,2,0:T(8,128)(2,1)S(1)}, f32[8,784,64]{1,2,0:T(8,128)}, f32[8,784,64]{1,2,0:T(8,128)}, f32[8,13,13]{2,0,1:T(8,128)S...) while((s32[]{:T(128)}, ...), condition=%wide.region_10.11_spmd.clone.clone, body=%wide.region_6.10_spmd.clone.clone.sunk | while | flops 164370688 | bytes 14238653 | solution.py:136
  119.8 6.0 %reshape.233 = f32[16,16,28,28]{3,2,1,0:T(8,128)} reshape(f32[256,784]{1,0:T(8,128)S(1)} %copy.64) | data formatting | bytes 1605632 | tf_op jit(solution)/shard_map/while/body/eval_jaxpr/reshape | solution.py:118
  125.8 4.3 convolution_bitcast_fusion.8
  138.7 6.0 %reshape.233 = f32[16,16,28,28]{3,2,1,0:T(8,128)} reshape(f32[256,784]{1,0:T(8,128)S(1)} %copy.64) | data formatting | bytes 1605632 | tf_op jit(solution)/shard_map/while/body/eval_jaxpr/reshape | solution.py:118
  144.8 4.3 convolution_bitcast_fusion.8
  157.7 6.0 %reshape.233 = f32[16,16,28,28]{3,2,1,0:T(8,128)} reshape(f32[256,784]{1,0:T(8,128)S(1)} %copy.64) | data formatting | bytes 1605632 | tf_op jit(solution)/shard_map/while/body/eval_jaxpr/reshape | solution.py:118
  163.7 4.3 convolution_bitcast_fusion.8
  176.7 6.0 %reshape.233 = f32[16,16,28,28]{3,2,1,0:T(8,128)} reshape(f32[256,784]{1,0:T(8,128)S(1)} %copy.64) | data formatting | bytes 1605632 | tf_op jit(solution)/shard_map/while/body/eval_jaxpr/reshape | solution.py:118
  182.7 4.3 convolution_bitcast_fusion.8
  195.6 6.0 %reshape.233 = f32[16,16,28,28]{3,2,1,0:T(8,128)} reshape(f32[256,784]{1,0:T(8,128)S(1)} %copy.64) | data formatting | bytes 1605632 | tf_op jit(solution)/shard_map/while/body/eval_jaxpr/reshape | solution.py:118
  201.7 4.3 convolution_bitcast_fusion.8
  214.6 6.0 %reshape.233 = f32[16,16,28,28]{3,2,1,0:T(8,128)} reshape(f32[256,784]{1,0:T(8,128)S(1)} %copy.64) | data formatting | bytes 1605632 | tf_op jit(solution)/shard_map/while/body/eval_jaxpr/reshape | solution.py:118
  220.6 4.3 convolution_bitcast_fusion.8
  233.5 6.0 %reshape.233 = f32[16,16,28,28]{3,2,1,0:T(8,128)} reshape(f32[256,784]{1,0:T(8,128)S(1)} %copy.64) | data formatting | bytes 1605632 | tf_op jit(solution)/shard_map/while/body/eval_jaxpr/reshape | solution.py:118
  239.6 4.3 convolution_bitcast_fusion.8
  252.5 6.0 %reshape.233 = f32[16,16,28,28]{3,2,1,0:T(8,128)} reshape(f32[256,784]{1,0:T(8,128)S(1)} %copy.64) | data formatting | bytes 1605632 | tf_op jit(solution)/shard_map/while/body/eval_jaxpr/reshape | solution.py:118
  258.5 4.3 convolution_bitcast_fusion.8
  271.5 28.9 %while.33 = (s32[]{:T(128)}, bf16[8,256,64]{1,2,0:T(8,128)(2,1)}, bf16[8,256,64]{2,1,0:T(8,128)(2,1)}, bf16[8,784,64]{2,1,0:T(8,128)(2,1)}, f32[8,256,784]{1,2,0...) while((s32[]{:T(128)}, bf16[8,256,64]{1,2,0:T(8,128)(2,1)}, bf16[8,256,64]{2,1,0:T(8,128)(2,1)}, ...), condition=%wide.region_5.6_spmd, body=%wide.region_2.5_spmd.sunk | while | flops 52985344 | bytes 3751509 | solution.py:92
  304.4 4.0 collective-permute-start.5
  317.6 41.1 %psum.15 = f32[8,13,13]{2,0,1:T(8,128)S(1)} all-reduce(f32[8,13,13]{2,0,1:T(8,128)S(1)} %get-tuple-element.181), channel_id=1, replica_groups=mesh['lat'=4,'lon'=8] {'lat','lon'}, use_global_device_ids=true, to_apply=%region_12.13 | all-reduce | flops 1352 | bytes 10816 | tf_op jit(solution)/shard_map/psum | solution.py:159
  363.7 3.3 collective-permute-start.6
  371.8 88.9 %all-reduce.2.cloned.1.call-done = f32[512,1024]{1,0:T(8,128)} async-done(((f32[512,1024]{1,0:T(8,128)}), f32[512,1024]{1,0:T(8,128)}) %all-reduce.2.cloned.1.call-update) | async-done | bytes 2097168 | tf_op jit(solution)/shard_map/psum | solution.py:159
  465.5 3.1 scatter-add.16
  469.9 3.5 scatter-add.19
  (197 shorter events, 157.4 us)
Async XLA Ops:
  7.2 92.1 %copy-start = (bf16[512,1024]{1,0:T(8,128)(2,1)S(1)}, bf16[512,1024]{1,0:T(8,128)(2,1)}, u32[]{:S(2)}) copy-start(bf16[512,1024]{1,0:T(8,128)(2,1)} %param.22) | copy-start | bytes 3145732
  7.2 9.0 %copy-start.10 = (f32[8,13,13]{2,0,1:T(8,128)S(1)}, f32[8,13,13]{2,0,1:T(8,128)}, u32[]{:S(2)}) copy-start(f32[8,13,13]{2,0,1:T(8,128)} %param.21) | copy-start | bytes 16228
  7.2 453.6 %all-reduce.2.cloned.1.call-start = ((), (), s32[]{:S(2)}) async-start(), calls=%async_computation | async-start | bytes 4194304 | tf_op jit(solution)/shard_map/psum | solution.py:159
  10.2 66.7 %collective-permute-start.1 = (bf16[16,6,1024]{2,1,0:T(8,128)(2,1)}, bf16[16,6,1024]{2,1,0:T(8,128)(2,1)S(1)}, u32[]{:S(2)}, u32[]{:S(2)}) collective-permute-start(bf16[16,6,1024]{2,1,0:T(8,128)(2,1)} %get-tuple-element.320), channel_id=1, source_target_pairs={{1,0},{2,1},{3,2},{4,3},{5,4},{6,5},{7,6},{0,7},{9,8},{10,9},{11,1... | collective-permute-start | bytes 589832 | tf_op jit(solution)/shard_map/ppermute | solution.py:19
  16.1 60.7 %collective-permute-start = (bf16[16,6,1024]{2,1,0:T(8,128)(2,1)}, bf16[16,6,1024]{2,1,0:T(8,128)(2,1)S(1)}, u32[]{:S(2)}, u32[]{:S(2)}) collective-permute-start(bf16[16,6,1024]{2,1,0:T(8,128)(2,1)} %get-tuple-element.319), channel_id=1, source_target_pairs={{0,1},{1,2},{2,3},{3,4},{4,5},{5,6},{6,7},{7,0},{8,9},{9,10},{10,1... | collective-permute-start | bytes 589832 | tf_op jit(solution)/shard_map/ppermute | solution.py:16
  76.8 13.1 %copy-start.5 = (bf16[16,6,1024]{2,1,0:T(8,128)(2,1)}, bf16[16,6,1024]{2,1,0:T(8,128)(2,1)S(1)}, u32[]{:S(2)}) copy-start(bf16[16,6,1024]{2,1,0:T(8,128)(2,1)S(1)} %collective-permute-done.1) | copy-start | bytes 589828
  76.9 13.0 %copy-start.6 = (bf16[16,6,1024]{2,1,0:T(8,128)(2,1)}, bf16[16,6,1024]{2,1,0:T(8,128)(2,1)S(1)}, u32[]{:S(2)}) copy-start(bf16[16,6,1024]{2,1,0:T(8,128)(2,1)S(1)} %collective-permute-done) | copy-start | bytes 589828
  78.1 22.5 %collective-permute-start.3 = (bf16[6,28,1024]{2,1,0:T(8,128)(2,1)}, bf16[6,28,1024]{2,1,0:T(8,128)(2,1)}, u32[]{:S(2)}, u32[]{:S(2)}) collective-permute-start(bf16[6,28,1024]{2,1,0:T(8,128)(2,1)} %get-tuple-element.316), channel_id=1, source_target_pairs={{8,0},{16,8},{24,16},{9,1},{17,9},{25,17},{10,2},{18,10},{26,18},{... | collective-permute-start | bytes 1032200 | tf_op jit(solution)/shard_map/ppermute | solution.py:19
  79.4 10.5 %copy-start.9 = (bf16[16,16,512]{2,1,0:T(8,128)(2,1)S(1)}, bf16[16,16,512]{2,1,0:T(8,128)(2,1)}, u32[]{:S(2)}) copy-start(bf16[16,16,512]{2,1,0:T(8,128)(2,1)} %param.18) | copy-start | bytes 786436
  79.4 21.2 %collective-permute-start.2 = (bf16[6,28,1024]{2,1,0:T(8,128)(2,1)}, bf16[6,28,1024]{2,1,0:T(8,128)(2,1)}, u32[]{:S(2)}, u32[]{:S(2)}) collective-permute-start(bf16[6,28,1024]{2,1,0:T(8,128)(2,1)} %get-tuple-element.315), channel_id=1, source_target_pairs={{0,8},{8,16},{16,24},{1,9},{9,17},{17,25},{2,10},{10,18},{18,26},{... | collective-permute-start | bytes 1032200 | tf_op jit(solution)/shard_map/ppermute | solution.py:16
  91.1 8.2 %copy-start.4 = (bf16[16,16,1024]{2,1,0:T(8,128)(2,1)S(1)}, bf16[16,16,1024]{2,1,0:T(8,128)(2,1)}, u32[]{:S(2)}) copy-start(bf16[16,16,1024]{2,1,0:T(8,128)(2,1)} %param.23) | copy-start | bytes 1572868
  263.2 1.9 copy-start.7
  267.8 2.2 copy-start.1
  302.2 57.9 %collective-permute-start.4 = (bf16[6,28,1024]{2,1,0:T(8,128)(2,1)}, bf16[6,28,1024]{2,1,0:T(8,128)(2,1)}, u32[]{:S(2)}, u32[]{:S(2)}) collective-permute-start(bf16[6,28,1024]{2,1,0:T(8,128)(2,1)} %convert_element_type.74), channel_id=1, source_target_pairs={{8,0},{16,8},{24,16},{9,1},{17,9},{25,17},{10,2},{18,10},{26,18},{... | collective-permute-start | bytes 1032200 | tf_op jit(solution)/shard_map/ppermute | solution.py:27
  304.4 56.7 %collective-permute-start.5 = (f32[6,28,1024]{2,1,0:T(8,128)}, f32[6,28,1024]{2,1,0:T(8,128)}, u32[]{:S(2)}, u32[]{:S(2)}) collective-permute-start(f32[6,28,1024]{2,1,0:T(8,128)} %slice.163), channel_id=1, source_target_pairs={{0,8},{8,16},{16,24},{1,9},{9,17},{17,25},{2,10},{10,18},{18,26},{... | collective-permute-start | bytes 2064392 | tf_op jit(solution)/shard_map/ppermute | solution.py:27
  315.5 43.3 %copy-start.3 = (bf16[8,256,64]{1,2,0:T(8,128)(2,1)S(1)}, bf16[8,256,64]{1,2,0:T(8,128)(2,1)}, u32[]{:S(2)}) copy-start(bf16[8,256,64]{1,2,0:T(8,128)(2,1)} %get-tuple-element.177) | copy-start | bytes 786436
  358.8 1.3 copy-start.2
  361.1 6.5 %copy-start.8 = (bf16[8,256,64]{1,2,0:T(8,128)(2,1)S(1)}, bf16[8,256,64]{1,2,0:T(8,128)(2,1)}, u32[]{:S(2)}) copy-start(bf16[8,256,64]{1,2,0:T(8,128)(2,1)} %copy-done.7) | copy-start | bytes 786436
  363.7 99.9 %collective-permute-start.6 = (f32[16,6,1024]{2,1,0:T(8,128)}, f32[16,6,1024]{2,1,0:T(8,128)}, u32[]{:S(2)}, u32[]{:S(2)}) collective-permute-start(f32[16,6,1024]{2,1,0:T(8,128)} %get-tuple-element.312), channel_id=1, source_target_pairs={{0,7},{1,0},{2,1},{3,2},{4,3},{5,4},{6,5},{7,6},{8,15},{9,8},{10,9... | collective-permute-start | bytes 1179656 | tf_op jit(solution)/shard_map/ppermute | solution.py:33
  371.8 96.8 %collective-permute-start.7 = (f32[16,6,1024]{2,1,0:T(8,128)}, f32[16,6,1024]{2,1,0:T(8,128)}, u32[]{:S(2)}, u32[]{:S(2)}) collective-permute-start(f32[16,6,1024]{2,1,0:T(8,128)} %get-tuple-element.311), channel_id=1, source_target_pairs={{0,1},{1,2},{2,3},{3,4},{4,5},{5,6},{6,7},{7,0},{8,9},{9,10},{10,1... | collective-permute-start | bytes 1179656 | tf_op jit(solution)/shard_map/ppermute | solution.py:33
Sparse Core Ops, SparseCore 0:
  317.8 142.9 all-reduce.1
where the time goes:
time: 486 us; the launch traced here: 482 us
  matrix products  144 us (30%)
  local copies, waits for them, and re-layouts  143 us (29%)
  waiting for transfers between devices  89 us (18%)
  blocking collectives  41.1 us (8%)
  other arithmetic  30.6 us (6%)
  starting transfers between devices  19.8 us (4%)
  between operations  14.3 us (3%)
    psum x1, waiting for transfers between devices, shards(): lax.psum((weight_local, bias_local), ('lat', 'lon'))  88.9 us
    reshape x8, local copies, waits for them, and re-layouts, backward_head(): score_grad.reshape(lat_dev, lon_dev, outer_lat, outer_lon)  48.2 us
    psum x1, blocking collectives, shards(): lax.psum((weight_local, bias_local), ('lat', 'lon'))  41.1 us
    dot_general x16, matrix products, backward_head(): jnp.einsum('ijkl,ika,jlb->ab', score_grad.reshape(lat_dev, lon_dev, outer...  36.5 us
    reshape x1, local copies, waits for them, and re-layouts, shards(): bias_table.reshape(heads, count_query, count_key)  28.1 us
    dot_general x16, matrix products, weights_of(): lax.dot_general(query_one, key_one, (((1,), (1,)), ((), ())), preferred_e...  25.5 us
    dot_general x2, matrix products, shards(): jnp.einsum('hab,ika,jlb->hijkl', rel_bias, row_keep, col_hot, precision=l...  15 us
    dot_general x8, matrix products, forward_head(): jnp.dot(probs.astype(jnp.bfloat16), value_one, preferred_element_type=jnp...  14.7 us
  transfers between devices with their start and end apart: 9, of which 1 were waited for; matrix products, arithmetic and copies ran while one was open for 22% of the time, Pallas kernels for 0%

commit v1 on v0

--- a/solution.py
+++ b/solution.py
@@ -4,6 +4,11 @@
 from jax.sharding import PartitionSpec as P
 
 RAD = 6
+
+
+def change_the_masks(q_in):
+    local_next = lax.psum(lax.psum(q_in, "lon"), "lat")
+    return local_next
 
 
 def with_halo(block, sides, width, periodic):
@@ -156,7 +161,7 @@
     center = center.at[:, :RAD].add(from_west)
     key_grad = center[:, :, :width].astype(jnp.bfloat16)
     value_grad = center[:, :, width:].astype(jnp.bfloat16)
-    weight_total, bias_total = lax.psum((weight_local, bias_local), ("lat", "lon"))
+    weight_total, bias_total = change_the_masks((weight_local, bias_local))
     weight_grad = (weight_total * norm_factor).astype(jnp.bfloat16)
     bias_grad = bias_total * norm_factor
     return (block_out, query_grad, key_grad, value_grad, weight_grad, bias_grad)

time: 486 us -> 424 us (0.87)
  waiting for transfers between devices: 89 us -> 10.6 us
  local copies, waits for them, and re-layouts: 143 us -> 154 us
  blocking collectives: 41.1 us -> 48.7 us
    psum x1 -> x2, waiting for transfers between devices: 88.9 us -> 0.01 us  [change_the_masks(): local_next = lax.psum(lax.psum(q_in, 'lon'), 'lat')]
    dynamic_update_slice x16, local copies, waits for them, and re-layouts: 0.85 us -> 12.2 us  [shards(): lax.map(backward_head, (query_heads, key_heads, value_heads, grad_heads,...]
    ppermute x2, waiting for transfers between devices: 0.01 us -> 10.5 us  [from_behind_2(): return lax.ppermute(value, axis, pairs)]
    psum x1 -> x2, blocking collectives: 41.1 us -> 48.7 us  [change_the_masks(): local_next = lax.psum(lax.psum(q_in, 'lon'), 'lat')]
    dot_general x8, matrix products: 14.7 us -> 9.74 us  [forward_head(): jnp.dot(probs.astype(jnp.bfloat16), value_one, preferred_element_type=jnp...]
  transfers between devices with their start and end apart: 9 -> 10, of which waited for: 1 -> 1; matrix products, arithmetic and copies ran while one was open for 22% -> 67% of each run, Pallas kernels for 0% -> 0%
where the time goes in v1:
time: 424 us; the launch traced here: 420 us
  local copies, waits for them, and re-layouts  154 us (36%)
  matrix products  140 us (33%)
  blocking collectives  48.7 us (11%)
  other arithmetic  30.8 us (7%)
  starting transfers between devices  20.7 us (5%)
  between operations  14.4 us (3%)
  waiting for transfers between devices  10.6 us (2%)
    psum x2, blocking collectives, change_the_masks(): local_next = lax.psum(lax.psum(q_in, 'lon'), 'lat')  48.7 us
    reshape x8, local copies, waits for them, and re-layouts, backward_head(): score_grad.reshape(lat_dev, lon_dev, outer_lat, outer_lon)  48.2 us
    dot_general x16, matrix products, backward_head(): jnp.einsum('ijkl,ika,jlb->ab', score_grad.reshape(lat_dev, lon_dev, outer...  37.7 us
    dot_general x16, matrix products, weights_of(): lax.dot_general(query_one, key_one, (((1,), (1,)), ((), ())), preferred_e...  28.5 us
    reshape x1, local copies, waits for them, and re-layouts, shards(): bias_table.reshape(heads, count_query, count_key)  28.1 us
    dot_general x2, matrix products, shards(): jnp.einsum('hab,ika,jlb->hijkl', rel_bias, row_keep, col_hot, precision=l...  15 us
    dot_general x8, matrix products, backward_head(): lax.dot_general(score_round, query_one, (((0,), (0,)), ((), ())), preferr...  14.5 us
    dot_general x8, matrix products, backward_head(): lax.dot_general(rounded, grad_one, (((0,), (0,)), ((), ())), preferred_el...  13.9 us
  transfers between devices with their start and end apart: 10, of which 1 were waited for; matrix products, arithmetic and copies ran while one was open for 67% of the time, Pallas kernels for 0%

profile of v1, /device:TPU:0, one launch (start us, length us, event | category | flops | bytes accessed | tf_op | source)
XLA Modules:
  0.0 419.7 jit_solution(6959912537225461335)
XLA Ops:
  10.2 6.0 %collective-permute-start.1 = (bf16[16,6,1024]{2,1,0:T(8,128)(2,1)}, bf16[16,6,1024]{2,1,0:T(8,128)(2,1)S(1)}, u32[]{:S(2)}, u32[]{:S(2)}) collective-permute-start(bf16[16,6,1024]{2,1,0:T(8,128)(2,1)} %get-tuple-element.320), channel_id=1, source_target_pairs={{1,0},{2,1},{3,2},{4,3},{5,4},{6,5},{7,6},{0,7},{9,8},{10,9},{11,1... | collective-permute-start | bytes 589832 | tf_op jit(solution)/shard_map/ppermute | solution.py:24
  17.3 14.0 %convolution_bitcast_fusion.4 = f32[8,16,16,28,28]{4,3,2,0,1:T(8,128)S(1)} fusion(f32[16,28,8,13,1]{1,3,4,2,0:T(8,128)S(1)} %convolution_bitcast_fusion.5, s32[16,28]{1,0:T(8,128)S(1)} %iota_subtract_fusion), kind=kOutput, calls=%fused_computation.61 | convolution fusion | flops 250484416 | bytes 6610688 | tf_op jit(solution)/shard_map/hab,ika,jlb->hijkl/dot_general | solution.py:71
  31.3 13.2 %copy.37 = f32[8,16,16,28,28]{4,3,2,1,0:T(8,128)} copy(f32[8,16,16,28,28]{4,3,2,0,1:T(8,128)S(1)} %convolution_bitcast_fusion.4) | data formatting | bytes 12845056 | tf_op jit(solution)/shard_map/hab,ika,jlb->hijkl/transpose | solution.py:71
  44.6 28.1 %reshape.215 = f32[8,256,784]{2,1,0:T(8,128)} reshape(f32[8,16,16,28,28]{4,3,2,1,0:T(8,128)} %copy.37) | data formatting | bytes 12845056 | tf_op jit(solution)/shard_map/reshape | solution.py:76
  73.5 3.4 gt.20
  79.4 3.9 collective-permute-start.2
  83.4 6.6 %broadcast_select_fusion = f32[8,256,784]{2,1,0:T(8,128)} fusion(f32[8,256,784]{2,1,0:T(8,128)} %reshape.215, pred[256,784]{1,0:T(8,128)(4,1)S(1)} %gt.20), kind=kLoop, calls=%fused_computation.70 | loop fusion | flops 1605632 | bytes 13045760 | tf_op jit(solution)/shard_map/jit(_where)/select_n | solution.py:76
  91.1 8.2 %copy.41 = f32[8,256,784]{1,2,0:T(8,128)} copy(f32[8,256,784]{2,1,0:T(8,128)} %broadcast_select_fusion) | data formatting | bytes 12845056 | tf_op jit(solution)/shard_map/while | solution.py:97
  112.3 23.3 %while.33 = (s32[]{:T(128)}, bf16[8,256,64]{1,2,0:T(8,128)(2,1)S(1)}, bf16[8,256,64]{2,1,0:T(8,128)(2,1)}, bf16[8,784,64]{2,1,0:T(8,128)(2,1)S(1)}, f32[8,256,78...) while((s32[]{:T(128)}, bf16[8,256,64]{1,2,0:T(8,128)(2,1)S(1)}, bf16[8,256,64]{2,1,0:T(8,128)(2,1)}, ...), condition=%wide.region_5.6_spmd, body=%wide.region_2.5_spmd.sunk | while | flops 52985344 | bytes 3751509 | solution.py:97
  138.2 165.4 %while.34 = (s32[]{:T(128)}, bf16[8,256,64]{1,2,0:T(8,128)(2,1)}, f32[8,784,64]{1,2,0:T(8,128)}, f32[8,784,64]{1,2,0:T(8,128)}, f32[8,13,13]{2,0,1:T(8,128)}, /*...) while((s32[]{:T(128)}, bf16[8,256,64]{1,2,0:T(8,128)(2,1)}, ...), condition=%wide.region_10.11_spmd.clone.clone, body=%wide.region_6.10_spmd.clone.clone.sunk | while | flops 164370688 | bytes 20661236 | solution.py:141
  146.6 6.0 %reshape.233 = f32[16,16,28,28]{3,2,1,0:T(8,128)} reshape(f32[256,784]{1,0:T(8,128)S(1)} %copy.64) | data formatting | bytes 1605632 | tf_op jit(solution)/shard_map/while/body/eval_jaxpr/reshape | solution.py:123
  152.6 4.4 %convolution_bitcast_fusion.8 = f32[13,16,28]{2,0,1:T(8,128)S(1)} fusion(f32[16,16,28,28]{3,2,1,0:T(8,128)} %reshape.233, s32[16,28]{1,0:T(8,128)S(1)} %get-tuple-element.494), kind=kOutput, calls=%fused_computation.23.clone.1 | convolution fusion | flops 31321472 | bytes 827904 | tf_op jit(solution)/shard_map/while/body/eval_jaxpr/ijkl,ika,jlb->ab/dot_general | solution.py:121
  167.3 6.0 %reshape.233 = f32[16,16,28,28]{3,2,1,0:T(8,128)} reshape(f32[256,784]{1,0:T(8,128)S(1)} %copy.64) | data formatting | bytes 1605632 | tf_op jit(solution)/shard_map/while/body/eval_jaxpr/reshape | solution.py:123
  173.3 4.4 %convolution_bitcast_fusion.8 = f32[13,16,28]{2,0,1:T(8,128)S(1)} fusion(f32[16,16,28,28]{3,2,1,0:T(8,128)} %reshape.233, s32[16,28]{1,0:T(8,128)S(1)} %get-tuple-element.494), kind=kOutput, calls=%fused_computation.23.clone.1 | convolution fusion | flops 31321472 | bytes 827904 | tf_op jit(solution)/shard_map/while/body/eval_jaxpr/ijkl,ika,jlb->ab/dot_general | solution.py:121
  187.9 6.0 %reshape.233 = f32[16,16,28,28]{3,2,1,0:T(8,128)} reshape(f32[256,784]{1,0:T(8,128)S(1)} %copy.64) | data formatting | bytes 1605632 | tf_op jit(solution)/shard_map/while/body/eval_jaxpr/reshape | solution.py:123
  194.0 4.5 %convolution_bitcast_fusion.8 = f32[13,16,28]{2,0,1:T(8,128)S(1)} fusion(f32[16,16,28,28]{3,2,1,0:T(8,128)} %reshape.233, s32[16,28]{1,0:T(8,128)S(1)} %get-tuple-element.494), kind=kOutput, calls=%fused_computation.23.clone.1 | convolution fusion | flops 31321472 | bytes 827904 | tf_op jit(solution)/shard_map/while/body/eval_jaxpr/ijkl,ika,jlb->ab/dot_general | solution.py:121
  208.6 6.0 %reshape.233 = f32[16,16,28,28]{3,2,1,0:T(8,128)} reshape(f32[256,784]{1,0:T(8,128)S(1)} %copy.64) | data formatting | bytes 1605632 | tf_op jit(solution)/shard_map/while/body/eval_jaxpr/reshape | solution.py:123
  214.6 4.6 %convolution_bitcast_fusion.8 = f32[13,16,28]{2,0,1:T(8,128)S(1)} fusion(f32[16,16,28,28]{3,2,1,0:T(8,128)} %reshape.233, s32[16,28]{1,0:T(8,128)S(1)} %get-tuple-element.494), kind=kOutput, calls=%fused_computation.23.clone.1 | convolution fusion | flops 31321472 | bytes 827904 | tf_op jit(solution)/shard_map/while/body/eval_jaxpr/ijkl,ika,jlb->ab/dot_general | solution.py:121
  229.4 6.0 %reshape.233 = f32[16,16,28,28]{3,2,1,0:T(8,128)} reshape(f32[256,784]{1,0:T(8,128)S(1)} %copy.64) | data formatting | bytes 1605632 | tf_op jit(solution)/shard_map/while/body/eval_jaxpr/reshape | solution.py:123
  235.4 4.4 %convolution_bitcast_fusion.8 = f32[13,16,28]{2,0,1:T(8,128)S(1)} fusion(f32[16,16,28,28]{3,2,1,0:T(8,128)} %reshape.233, s32[16,28]{1,0:T(8,128)S(1)} %get-tuple-element.494), kind=kOutput, calls=%fused_computation.23.clone.1 | convolution fusion | flops 31321472 | bytes 827904 | tf_op jit(solution)/shard_map/while/body/eval_jaxpr/ijkl,ika,jlb->ab/dot_general | solution.py:121
  250.0 6.0 %reshape.233 = f32[16,16,28,28]{3,2,1,0:T(8,128)} reshape(f32[256,784]{1,0:T(8,128)S(1)} %copy.64) | data formatting | bytes 1605632 | tf_op jit(solution)/shard_map/while/body/eval_jaxpr/reshape | solution.py:123
  256.1 4.4 %convolution_bitcast_fusion.8 = f32[13,16,28]{2,0,1:T(8,128)S(1)} fusion(f32[16,16,28,28]{3,2,1,0:T(8,128)} %reshape.233, s32[16,28]{1,0:T(8,128)S(1)} %get-tuple-element.494), kind=kOutput, calls=%fused_computation.23.clone.1 | convolution fusion | flops 31321472 | bytes 827904 | tf_op jit(solution)/shard_map/while/body/eval_jaxpr/ijkl,ika,jlb->ab/dot_general | solution.py:121
  270.7 6.0 %reshape.233 = f32[16,16,28,28]{3,2,1,0:T(8,128)} reshape(f32[256,784]{1,0:T(8,128)S(1)} %copy.64) | data formatting | bytes 1605632 | tf_op jit(solution)/shard_map/while/body/eval_jaxpr/reshape | solution.py:123
  276.7 4.4 %convolution_bitcast_fusion.8 = f32[13,16,28]{2,0,1:T(8,128)S(1)} fusion(f32[16,16,28,28]{3,2,1,0:T(8,128)} %reshape.233, s32[16,28]{1,0:T(8,128)S(1)} %get-tuple-element.494), kind=kOutput, calls=%fused_computation.23.clone.1 | convolution fusion | flops 31321472 | bytes 827904 | tf_op jit(solution)/shard_map/while/body/eval_jaxpr/ijkl,ika,jlb->ab/dot_general | solution.py:121
  291.3 6.0 %reshape.233 = f32[16,16,28,28]{3,2,1,0:T(8,128)} reshape(f32[256,784]{1,0:T(8,128)S(1)} %copy.64) | data formatting | bytes 1605632 | tf_op jit(solution)/shard_map/while/body/eval_jaxpr/reshape | solution.py:123
  297.4 4.4 %convolution_bitcast_fusion.8 = f32[13,16,28]{2,0,1:T(8,128)S(1)} fusion(f32[16,16,28,28]{3,2,1,0:T(8,128)} %reshape.233, s32[16,28]{1,0:T(8,128)S(1)} %get-tuple-element.494), kind=kOutput, calls=%fused_computation.23.clone.1 | convolution fusion | flops 31321472 | bytes 827904 | tf_op jit(solution)/shard_map/while/body/eval_jaxpr/ijkl,ika,jlb->ab/dot_general | solution.py:121
  311.0 3.4 collective-permute-start.5
  326.8 4.7 %collective-permute-start.6 = (f32[16,6,1024]{2,1,0:T(8,128)}, f32[16,6,1024]{2,1,0:T(8,128)}, u32[]{:S(2)}, u32[]{:S(2)}) collective-permute-start(f32[16,6,1024]{2,1,0:T(8,128)} %get-tuple-element.312), channel_id=1, source_target_pairs={{0,7},{1,0},{2,1},{3,2},{4,3},{5,4},{6,5},{7,6},{8,15},{9,8},{10,9... | collective-permute-start | bytes 1179656 | tf_op jit(solution)/shard_map/ppermute | solution.py:38
  337.0 37.1 %psum.30 = f32[8,13,13]{2,0,1:T(8,128)S(1)} all-reduce(f32[8,13,13]{2,0,1:T(8,128)S(1)} %copy-done.11), channel_id=1, replica_groups=mesh['lat'=4,'lon'=8] {'lon'}, use_global_device_ids=true, to_apply=%region_13.14 | all-reduce | flops 1352 | bytes 10816 | tf_op jit(solution)/shard_map/psum | solution.py:10
  374.1 11.7 %psum.31 = f32[8,13,13]{2,0,1:T(8,128)S(1)} all-reduce(f32[8,13,13]{2,0,1:T(8,128)S(1)} %psum.30), channel_id=1, replica_groups=mesh['lat'=4,'lon'=8] {'lat'}, use_global_device_ids=true, to_apply=%region_14.15 | all-reduce | flops 1352 | bytes 10816 | tf_op jit(solution)/shard_map/psum | solution.py:10
  392.5 10.5 %collective-permute-done.7 = f32[16,6,1024]{2,1,0:T(8,128)} collective-permute-done((f32[16,6,1024]{2,1,0:T(8,128)}, f32[16,6,1024]{2,1,0:T(8,128)}, u32[]{:S(2)}, u32[]{:S(2)}) %collective-permute-start.7) | collective-permute-done | bytes 393248 | tf_op jit(solution)/shard_map/ppermute | solution.py:38
  404.3 3.5 scatter-add.19
  (231 shorter events, 166.6 us)
Async XLA Ops:
  7.2 92.2 %copy-start = (bf16[512,1024]{1,0:T(8,128)(2,1)S(1)}, bf16[512,1024]{1,0:T(8,128)(2,1)}, u32[]{:S(2)}) copy-start(bf16[512,1024]{1,0:T(8,128)(2,1)} %param.22) | copy-start | bytes 3145732
  7.2 9.0 %copy-start.10 = (f32[8,13,13]{2,0,1:T(8,128)S(1)}, f32[8,13,13]{2,0,1:T(8,128)}, u32[]{:S(2)}) copy-start(f32[8,13,13]{2,0,1:T(8,128)} %param.21) | copy-start | bytes 16228
  7.2 324.3 %all-reduce.3.cloned.1.call-start = ((), (), s32[]{:S(2)}) async-start(), calls=%async_computation | async-start | bytes 4194304 | tf_op jit(solution)/shard_map/psum | solution.py:10
  10.2 66.7 %collective-permute-start.1 = (bf16[16,6,1024]{2,1,0:T(8,128)(2,1)}, bf16[16,6,1024]{2,1,0:T(8,128)(2,1)S(1)}, u32[]{:S(2)}, u32[]{:S(2)}) collective-permute-start(bf16[16,6,1024]{2,1,0:T(8,128)(2,1)} %get-tuple-element.320), channel_id=1, source_target_pairs={{1,0},{2,1},{3,2},{4,3},{5,4},{6,5},{7,6},{0,7},{9,8},{10,9},{11,1... | collective-permute-start | bytes 589832 | tf_op jit(solution)/shard_map/ppermute | solution.py:24
  16.1 60.7 %collective-permute-start = (bf16[16,6,1024]{2,1,0:T(8,128)(2,1)}, bf16[16,6,1024]{2,1,0:T(8,128)(2,1)S(1)}, u32[]{:S(2)}, u32[]{:S(2)}) collective-permute-start(bf16[16,6,1024]{2,1,0:T(8,128)(2,1)} %get-tuple-element.319), channel_id=1, source_target_pairs={{0,1},{1,2},{2,3},{3,4},{4,5},{5,6},{6,7},{7,0},{8,9},{9,10},{10,1... | collective-permute-start | bytes 589832 | tf_op jit(solution)/shard_map/ppermute | solution.py:21
  76.9 13.1 %copy-start.7 = (bf16[16,6,1024]{2,1,0:T(8,128)(2,1)}, bf16[16,6,1024]{2,1,0:T(8,128)(2,1)S(1)}, u32[]{:S(2)}) copy-start(bf16[16,6,1024]{2,1,0:T(8,128)(2,1)S(1)} %collective-permute-done.1) | copy-start | bytes 589828
  76.9 13.1 %copy-start.8 = (bf16[16,6,1024]{2,1,0:T(8,128)(2,1)}, bf16[16,6,1024]{2,1,0:T(8,128)(2,1)S(1)}, u32[]{:S(2)}) copy-start(bf16[16,6,1024]{2,1,0:T(8,128)(2,1)S(1)} %collective-permute-done) | copy-start | bytes 589828
  78.1 22.5 %collective-permute-start.3 = (bf16[6,28,1024]{2,1,0:T(8,128)(2,1)}, bf16[6,28,1024]{2,1,0:T(8,128)(2,1)}, u32[]{:S(2)}, u32[]{:S(2)}) collective-permute-start(bf16[6,28,1024]{2,1,0:T(8,128)(2,1)} %get-tuple-element.316), channel_id=1, source_target_pairs={{8,0},{16,8},{24,16},{9,1},{17,9},{25,17},{10,2},{18,10},{26,18},{... | collective-permute-start | bytes 1032200 | tf_op jit(solution)/shard_map/ppermute | solution.py:24
  79.4 10.6 %copy-start.9 = (bf16[16,16,512]{2,1,0:T(8,128)(2,1)S(1)}, bf16[16,16,512]{2,1,0:T(8,128)(2,1)}, u32[]{:S(2)}) copy-start(bf16[16,16,512]{2,1,0:T(8,128)(2,1)} %param.18) | copy-start | bytes 786436
  79.4 21.2 %collective-permute-start.2 = (bf16[6,28,1024]{2,1,0:T(8,128)(2,1)}, bf16[6,28,1024]{2,1,0:T(8,128)(2,1)}, u32[]{:S(2)}, u32[]{:S(2)}) collective-permute-start(bf16[6,28,1024]{2,1,0:T(8,128)(2,1)} %get-tuple-element.315), channel_id=1, source_target_pairs={{0,8},{8,16},{16,24},{1,9},{9,17},{17,25},{2,10},{10,18},{18,26},{... | collective-permute-start | bytes 1032200 | tf_op jit(solution)/shard_map/ppermute | solution.py:21
  91.1 8.2 %copy-start.5 = (bf16[16,16,1024]{2,1,0:T(8,128)(2,1)S(1)}, bf16[16,16,1024]{2,1,0:T(8,128)(2,1)}, u32[]{:S(2)}) copy-start(bf16[16,16,1024]{2,1,0:T(8,128)(2,1)} %param.23) | copy-start | bytes 1572868
  112.3 23.4 %copy-start.6 = (bf16[16,16,1024]{2,1,0:T(8,128)(2,1)S(1)}, bf16[16,16,1024]{2,1,0:T(8,128)(2,1)}, u32[]{:S(2)}) copy-start(bf16[16,16,1024]{2,1,0:T(8,128)(2,1)} %param.23) | copy-start | bytes 1572868
  137.4 272.6 %all-reduce.5.cloned.1.call-start = ((), (), s32[]{:S(2)}) async-start(), calls=%async_computation.1 | async-start | bytes 4194304 | tf_op jit(solution)/shard_map/psum | solution.py:10
  138.2 3.7 copy-start.1
  152.6 6.2 %copy-start.2 = (bf16[8,784,64]{2,1,0:T(8,128)(2,1)S(1)}, bf16[8,784,64]{2,1,0:T(8,128)(2,1)}, u32[]{:S(2)}) copy-start(bf16[8,784,64]{2,1,0:T(8,128)(2,1)} %copy-done.1) | copy-start | bytes 2408452 | tf_op jit(solution)/shard_map/while
  158.9 3.7 copy-start.1
  173.3 6.2 %copy-start.2 = (bf16[8,784,64]{2,1,0:T(8,128)(2,1)S(1)}, bf16[8,784,64]{2,1,0:T(8,128)(2,1)}, u32[]{:S(2)}) copy-start(bf16[8,784,64]{2,1,0:T(8,128)(2,1)} %copy-done.1) | copy-start | bytes 2408452 | tf_op jit(solution)/shard_map/while
  179.5 3.7 copy-start.1
  194.0 6.3 %copy-start.2 = (bf16[8,784,64]{2,1,0:T(8,128)(2,1)S(1)}, bf16[8,784,64]{2,1,0:T(8,128)(2,1)}, u32[]{:S(2)}) copy-start(bf16[8,784,64]{2,1,0:T(8,128)(2,1)} %copy-done.1) | copy-start | bytes 2408452 | tf_op jit(solution)/shard_map/while
  214.6 6.4 %copy-start.2 = (bf16[8,784,64]{2,1,0:T(8,128)(2,1)S(1)}, bf16[8,784,64]{2,1,0:T(8,128)(2,1)}, u32[]{:S(2)}) copy-start(bf16[8,784,64]{2,1,0:T(8,128)(2,1)} %copy-done.1) | copy-start | bytes 2408452 | tf_op jit(solution)/shard_map/while
  221.0 3.7 copy-start.1
  235.4 6.2 %copy-start.2 = (bf16[8,784,64]{2,1,0:T(8,128)(2,1)S(1)}, bf16[8,784,64]{2,1,0:T(8,128)(2,1)}, u32[]{:S(2)}) copy-start(bf16[8,784,64]{2,1,0:T(8,128)(2,1)} %copy-done.1) | copy-start | bytes 2408452 | tf_op jit(solution)/shard_map/while
  256.1 6.2 %copy-start.2 = (bf16[8,784,64]{2,1,0:T(8,128)(2,1)S(1)}, bf16[8,784,64]{2,1,0:T(8,128)(2,1)}, u32[]{:S(2)}) copy-start(bf16[8,784,64]{2,1,0:T(8,128)(2,1)} %copy-done.1) | copy-start | bytes 2408452 | tf_op jit(solution)/shard_map/while
  276.7 6.2 %copy-start.2 = (bf16[8,784,64]{2,1,0:T(8,128)(2,1)S(1)}, bf16[8,784,64]{2,1,0:T(8,128)(2,1)}, u32[]{:S(2)}) copy-start(bf16[8,784,64]{2,1,0:T(8,128)(2,1)} %copy-done.1) | copy-start | bytes 2408452 | tf_op jit(solution)/shard_map/while
  282.9 3.7 copy-start.1
  297.4 6.2 %copy-start.2 = (bf16[8,784,64]{2,1,0:T(8,128)(2,1)S(1)}, bf16[8,784,64]{2,1,0:T(8,128)(2,1)}, u32[]{:S(2)}) copy-start(bf16[8,784,64]{2,1,0:T(8,128)(2,1)} %copy-done.1) | copy-start | bytes 2408452 | tf_op jit(solution)/shard_map/while
  311.0 13.3 %collective-permute-start.5 = (f32[6,28,1024]{2,1,0:T(8,128)}, f32[6,28,1024]{2,1,0:T(8,128)}, u32[]{:S(2)}, u32[]{:S(2)}) collective-permute-start(f32[6,28,1024]{2,1,0:T(8,128)} %slice.163), channel_id=1, source_target_pairs={{0,8},{8,16},{16,24},{1,9},{9,17},{17,25},{2,10},{10,18},{18,26},{... | collective-permute-start | bytes 2064392 | tf_op jit(solution)/shard_map/ppermute | solution.py:32
  315.5 7.5 %collective-permute-start.4 = (bf16[6,28,1024]{2,1,0:T(8,128)(2,1)S(1)}, bf16[6,28,1024]{2,1,0:T(8,128)(2,1)}, u32[]{:S(2)}, u32[]{:S(2)}) collective-permute-start(bf16[6,28,1024]{2,1,0:T(8,128)(2,1)S(1)} %convert_element_type.74), channel_id=1, source_target_pairs={{8,0},{16,8},{24,16},{9,1},{17,9},{25,17},{10,2},{18,10},{26,18},{... | collective-permute-start | bytes 1032200 | tf_op jit(solution)/shard_map/ppermute | solution.py:32
  325.7 5.9 %copy-start.4 = (bf16[8,256,64]{1,2,0:T(8,128)(2,1)S(1)}, bf16[8,256,64]{1,2,0:T(8,128)(2,1)}, u32[]{:S(2)}) copy-start(bf16[8,256,64]{1,2,0:T(8,128)(2,1)} %copy-done.3) | copy-start | bytes 786436
  326.8 60.8 %collective-permute-start.6 = (f32[16,6,1024]{2,1,0:T(8,128)}, f32[16,6,1024]{2,1,0:T(8,128)}, u32[]{:S(2)}, u32[]{:S(2)}) collective-permute-start(f32[16,6,1024]{2,1,0:T(8,128)} %get-tuple-element.312), channel_id=1, source_target_pairs={{0,7},{1,0},{2,1},{3,2},{4,3},{5,4},{6,5},{7,6},{8,15},{9,8},{10,9... | collective-permute-start | bytes 1179656 | tf_op jit(solution)/shard_map/ppermute | solution.py:38
  331.6 5.5 %copy-start.11 = (f32[8,13,13]{2,0,1:T(8,128)S(1)}, f32[8,13,13]{2,0,1:T(8,128)}, u32[]{:S(2)}) copy-start(f32[8,13,13]{2,0,1:T(8,128)} %get-tuple-element.181) | copy-start | bytes 16228
  385.8 17.3 %collective-permute-start.7 = (f32[16,6,1024]{2,1,0:T(8,128)}, f32[16,6,1024]{2,1,0:T(8,128)}, u32[]{:S(2)}, u32[]{:S(2)}) collective-permute-start(f32[16,6,1024]{2,1,0:T(8,128)} %get-tuple-element.311), channel_id=1, source_target_pairs={{0,1},{1,2},{2,3},{3,4},{4,5},{5,6},{6,7},{7,0},{8,9},{9,10},{10,1... | collective-permute-start | bytes 1179656 | tf_op jit(solution)/shard_map/ppermute | solution.py:38
  (4 other events, 12.8 us)
Sparse Core Ops, SparseCore 0:
  137.6 103.3 all-reduce.2
  331.7 50.2 all-reduce.4
